TPU v7x, 32 devices: a whole 2x2x4 slice. The times are simulated.
32 devices in a mesh: dp: 8 (over y, x, core), tensor: 4 (over z).
Axes of the slice: x: 2, y: 2, z: 4, core: 2. Of those that a mesh axis runs over, the one named last changes fastest.
Arguments:
- inputs: bfloat16 [8, 1024, 2048], P('dp'), may hold values from -6 to 6
- segments: int32 [8, 1024], P('dp'), may hold values from 0 to 3, never falling along the last dimension, each value on 1 to 512 neighbouring positions
- cotangent: bfloat16 [8, 1024, 2048], P('dp'), may hold values from -6 to 6
- w_query: bfloat16 [2048, 2048], P(None, 'tensor'), may hold values from -0.046875 to 0.046875
- w_key: bfloat16 [2048, 2048], P(None, 'tensor'), may hold values from -0.046875 to 0.046875
- w_value: bfloat16 [2048, 2048], P(None, 'tensor'), may hold values from -0.125 to 0.125
- w_out: bfloat16 [2048, 2048], P('tensor'), may hold values from -0.5 to 0.5
- w_gate: bfloat16 [2048, 5120], P(None, 'tensor'), may hold values from -0.125 to 0.125
- w_up: bfloat16 [2048, 5120], P(None, 'tensor'), may hold values from -0.125 to 0.125
- w_down: bfloat16 [5120, 2048], P('tensor'), may hold values from -0.125 to 0.125
- gain_attn: float32 [2048], replicated, may hold values from 0.5 to 1.5
- gain_ffn: float32 [2048], replicated, may hold values from 0.5 to 1.5
- bias_table: float32 [32, 32], P(None, 'tensor'), may hold values from -4 to 4
Outputs:
- output: bfloat16 [8, 1024, 2048], P('dp', 'tensor')
- input_grad: bfloat16 [8, 1024, 2048], P('dp', 'tensor')
- query_grad: float32 [2048, 2048], P(None, 'tensor')
- key_grad: float32 [2048, 2048], P(None, 'tensor')
- value_grad: float32 [2048, 2048], P(None, 'tensor')
- out_grad: float32 [2048, 2048], P('tensor')
- gate_grad: float32 [2048, 5120], P(None, 'tensor')
- up_grad: float32 [2048, 5120], P(None, 'tensor')
- down_grad: float32 [5120, 2048], P('tensor')
- gain_attn_grad: float32 [2048], replicated
- gain_ffn_grad: float32 [2048], replicated
- table_grad: float32 [32, 32], P(None, 'tensor')
Inputs may be any that keep to these rules, and one draw needn't show every extreme that they name: `segments`: each row of 1024 tokens holds 4 documents one after another; document numbers never fall along a row; each document has 1 to 512 tokens and one in every row has exactly 512.
All inputs are finite; a program needn't handle non-finite values.
Results may differ from a plain program's by a relative error of at most 0.024.
Values may be sent and summed in bfloat16 or wider, within the bound.
A program may use at most 320 MiB of HBM per device.

v0:
```python
import jax
import jax.numpy as jnp
from jax import lax
from jax.sharding import PartitionSpec as P

thresholds = (12, 16, 23, 32, 46, 64, 91)
highest = lax.Precision.HIGHEST


def buckets_of(start_row, query_count, length):
    queries = start_row + jnp.arange(query_count, dtype=jnp.int32)
    targets = jnp.arange(length, dtype=jnp.int32)
    offset = targets[None, :] - queries[:, None]
    distance = jnp.abs(offset)
    far_bucket = jnp.full(distance.shape, 8, jnp.int32)
    for bound_value in thresholds:
        far_bucket = far_bucket + (distance >= bound_value).astype(jnp.int32)
    near_bucket = jnp.where(distance < 8, distance, far_bucket)
    return near_bucket + 16 * (offset > 0).astype(jnp.int32)


def bucket_onehot(start_row, query_count, length, bucket_count):
    bucket = buckets_of(start_row, query_count, length).reshape(1, query_count * length)
    labels = jnp.arange(bucket_count, dtype=jnp.int32)[:, None]
    return (bucket == labels).astype(jnp.float32)


def project(left_side, right_side):
    return jnp.dot(left_side, right_side, preferred_element_type=jnp.float32)


def project_back(left_side, right_side):
    return lax.dot_general(
        left_side, right_side, (((1,), (1,)), ((), ())), preferred_element_type=jnp.float32
    )


def weight_term(left_side, right_side):
    return lax.dot_general(
        left_side, right_side, (((0,), (0,)), ((), ())), preferred_element_type=jnp.float32
    )


def norm_scale(signal):
    return lax.rsqrt(jnp.mean(signal * signal, axis=-1, keepdims=True) + 1e-06)


def norm_back(signal, rms_scale, gain_vec, grad_normed):
    grad_hat = grad_normed * gain_vec
    inner_mean = jnp.mean(grad_hat * signal, axis=-1, keepdims=True)
    return rms_scale * (grad_hat - signal * rms_scale * rms_scale * inner_mean)


def gain_term(signal, rms_scale, grad_normed):
    return jnp.sum((grad_normed * signal * rms_scale).reshape(-1, signal.shape[-1]), axis=0)


def score_block(query_block, key_row, bias_block, same_doc):
    raw_scores = jnp.einsum(
        "qhd,khd->hqk", query_block, key_row, preferred_element_type=jnp.float32
    )
    return jnp.where(same_doc[None], raw_scores + bias_block, -1000000000.0)


def shards(
    inputs,
    segments,
    cotangent,
    w_query,
    w_key,
    w_value,
    w_out,
    w_gate,
    w_up,
    w_down,
    gain_attn,
    gain_ffn,
    bias_table,
):
    row_count, length, model_width = inputs.shape
    share_rows = length // lax.axis_size("tensor")
    first_row = lax.axis_index("tensor") * share_rows
    bucket_count, head_count = bias_table.shape
    local_width = w_query.shape[1]
    head_dim = local_width // head_count
    block_rows = min(512, length)
    block_count = length // block_rows
    token_count = row_count * length
    plane = (row_count, length, model_width)

    def take_share(signal):
        return lax.dynamic_slice_in_dim(signal, first_row, share_rows, 1)

    flat_inputs = inputs.reshape(token_count, model_width).astype(jnp.float32)
    scale_attn = norm_scale(flat_inputs)
    normed = (flat_inputs * scale_attn * gain_attn).astype(jnp.bfloat16)
    heads_shape = (row_count, length, head_count, head_dim)
    queries = project(normed, w_query).astype(jnp.bfloat16).reshape(heads_shape)
    key_proj = project(normed, w_key).astype(jnp.bfloat16).reshape(heads_shape)
    value_proj = project(normed, w_value).astype(jnp.bfloat16).reshape(heads_shape)
    table_heads = jnp.transpose(bias_table)
    bias_blocks = []
    for block_index in range(block_count):
        onehot = bucket_onehot(block_index * block_rows, block_rows, length, bucket_count)
        bias_flat = jnp.dot(table_heads, onehot, precision=highest)
        bias_blocks.append(bias_flat.reshape(head_count, block_rows, length))
    row_index = 0
    doc_row = segments[row_index]
    pieces = []
    totals_row = []
    for block_index in range(block_count):
        block_start = block_index * block_rows
        same_doc = doc_row[block_start : block_start + block_rows, None] == doc_row[None, :]
        query_block = queries[row_index, block_start : block_start + block_rows]
        scores = score_block(query_block, key_proj[row_index], bias_blocks[block_index], same_doc)
        row_max = jnp.max(scores, axis=-1, keepdims=True)
        weighted = jnp.exp(scores - row_max)
        row_total = jnp.sum(weighted, axis=-1, keepdims=True)
        softmaxed = (weighted / row_total).astype(jnp.bfloat16)
        totals_row.append(row_max + jnp.log(row_total))
        pieces.append(
            jnp.einsum(
                "hqk,khd->qhd", softmaxed, value_proj[row_index], preferred_element_type=jnp.float32
            ).astype(jnp.bfloat16)
        )
    log_totals = [totals_row]
    mixed_rows = [jnp.concatenate(pieces, axis=0)]
    mixed_heads = jnp.stack(mixed_rows).reshape(token_count, local_width)
    attn_part = project(mixed_heads, w_out)
    attn_total = lax.psum(attn_part.astype(jnp.bfloat16), "tensor").astype(jnp.float32)
    middle = flat_inputs + attn_total
    scale_ffn = norm_scale(middle)
    normed_ffn = (middle * scale_ffn * gain_ffn).astype(jnp.bfloat16)
    gate_pre = project(normed_ffn, w_gate)
    up_pre = project(normed_ffn, w_up)
    hidden = (jax.nn.gelu(gate_pre, approximate=True) * up_pre).astype(jnp.bfloat16)
    ffn_part = project(hidden, w_down)
    ffn_total = lax.psum(ffn_part.astype(jnp.bfloat16), "tensor").astype(jnp.float32)
    output = take_share((middle + ffn_total).reshape(plane)).astype(jnp.bfloat16)
    grad_out = cotangent.reshape(token_count, model_width)
    down_grad = weight_term(hidden, grad_out)
    grad_hidden = project_back(grad_out, w_down)
    normed_again = lax.optimization_barrier(normed_ffn)
    gate_back = project(normed_again, w_gate)
    up_back = project(normed_again, w_up)
    act_value, act_pull = jax.vjp(lambda signal: jax.nn.gelu(signal, approximate=True), gate_back)
    grad_gate = act_pull(grad_hidden * up_back)[0].astype(jnp.bfloat16)
    grad_up = (grad_hidden * act_value).astype(jnp.bfloat16)
    gate_grad = weight_term(normed_ffn, grad_gate)
    up_grad = weight_term(normed_ffn, grad_up)
    norm_ffn_part = project_back(grad_gate, w_gate) + project_back(grad_up, w_up)
    grad_normed_ffn = lax.psum(norm_ffn_part.astype(jnp.bfloat16), "tensor").astype(jnp.float32)
    grad_middle = grad_out.astype(jnp.float32) + norm_back(
        middle, scale_ffn, gain_ffn, grad_normed_ffn
    )
    gain_ffn_part = gain_term(
        take_share(middle.reshape(plane)),
        take_share(scale_ffn.reshape(row_count, length, 1)),
        take_share(grad_normed_ffn.reshape(plane)),
    )
    grad_branch = grad_middle.astype(jnp.bfloat16)
    out_grad = weight_term(mixed_heads, grad_branch)
    grad_mixed = project_back(grad_branch, w_out).astype(jnp.bfloat16).reshape(heads_shape)
    score_sums = [
        jnp.zeros((head_count, block_rows, length), jnp.float32)
        for block_index in range(block_count)
    ]
    row_index = 0
    doc_row = segments[row_index]
    key_row = key_proj[row_index]
    value_row = value_proj[row_index]
    key_sum = jnp.zeros((length, head_count, head_dim), jnp.float32)
    value_sum = jnp.zeros((length, head_count, head_dim), jnp.float32)
    query_pieces = []
    for block_index in range(block_count):
        block_start = block_index * block_rows
        same_doc = doc_row[block_start : block_start + block_rows, None] == doc_row[None, :]
        query_block = queries[row_index, block_start : block_start + block_rows]
        grad_block = grad_mixed[row_index, block_start : block_start + block_rows]
        scores = score_block(query_block, key_row, bias_blocks[block_index], same_doc)
        weights_back = jnp.exp(scores - log_totals[row_index][block_index])
        grad_weights = jnp.einsum(
            "qhd,khd->hqk", grad_block, value_row, preferred_element_type=jnp.float32
        )
        row_delta = jnp.sum(weights_back * grad_weights, axis=-1, keepdims=True)
        grad_scores = weights_back * (grad_weights - row_delta)
        score_sums[block_index] = grad_scores
        scores_low = grad_scores.astype(jnp.bfloat16)
        query_pieces.append(
            jnp.einsum(
                "hqk,khd->qhd", scores_low, key_row, preferred_element_type=jnp.float32
            ).astype(jnp.bfloat16)
        )
        key_sum = key_sum + jnp.einsum(
            "hqk,qhd->khd", scores_low, query_block, preferred_element_type=jnp.float32
        )
        value_sum = value_sum + jnp.einsum(
            "hqk,qhd->khd",
            weights_back.astype(jnp.bfloat16),
            grad_block,
            preferred_element_type=jnp.float32,
        )
    query_rows = [jnp.concatenate(query_pieces, axis=0)]
    key_rows = [key_sum.astype(jnp.bfloat16)]
    value_rows = [value_sum.astype(jnp.bfloat16)]
    grad_query = jnp.stack(query_rows).reshape(token_count, local_width)
    grad_key = jnp.stack(key_rows).reshape(token_count, local_width)
    grad_value = jnp.stack(value_rows).reshape(token_count, local_width)
    table_grad = jnp.zeros((bucket_count, head_count), jnp.float32)
    for block_index in range(block_count):
        onehot = bucket_onehot(block_index * block_rows, block_rows, length, bucket_count)
        table_grad = table_grad + lax.dot_general(
            onehot,
            score_sums[block_index].reshape(head_count, block_rows * length),
            (((1,), (1,)), ((), ())),
            precision=highest,
        )
    query_grad = weight_term(normed, grad_query)
    key_grad = weight_term(normed, grad_key)
    value_grad = weight_term(normed, grad_value)
    norm_attn_part = (
        project_back(grad_query, w_query)
        + project_back(grad_key, w_key)
        + project_back(grad_value, w_value)
    )
    grad_normed_attn = lax.psum(norm_attn_part.astype(jnp.bfloat16), "tensor").astype(jnp.float32)
    grad_input = grad_middle + norm_back(flat_inputs, scale_attn, gain_attn, grad_normed_attn)
    input_grad = take_share(grad_input.reshape(plane)).astype(jnp.bfloat16)
    gain_attn_part = gain_term(
        take_share(flat_inputs.reshape(plane)),
        take_share(scale_attn.reshape(row_count, length, 1)),
        take_share(grad_normed_attn.reshape(plane)),
    )
    gain_attn_grad, gain_ffn_grad = lax.psum((gain_attn_part, gain_ffn_part), ("dp", "tensor"))
    reduced = (
        lax.psum_scatter(
            query_grad.astype(jnp.bfloat16), "dp", scatter_dimension=0, tiled=True
        ).astype(jnp.float32),
        lax.psum_scatter(
            key_grad.astype(jnp.bfloat16), "dp", scatter_dimension=0, tiled=True
        ).astype(jnp.float32),
        lax.psum_scatter(
            value_grad.astype(jnp.bfloat16), "dp", scatter_dimension=0, tiled=True
        ).astype(jnp.float32),
        lax.psum_scatter(
            out_grad.astype(jnp.bfloat16), "dp", scatter_dimension=1, tiled=True
        ).astype(jnp.float32),
        lax.psum_scatter(
            gate_grad.astype(jnp.bfloat16), "dp", scatter_dimension=0, tiled=True
        ).astype(jnp.float32),
        lax.psum_scatter(
            up_grad.astype(jnp.bfloat16), "dp", scatter_dimension=0, tiled=True
        ).astype(jnp.float32),
        lax.psum_scatter(
            down_grad.astype(jnp.bfloat16), "dp", scatter_dimension=1, tiled=True
        ).astype(jnp.float32),
        lax.psum_scatter(
            table_grad.astype(jnp.bfloat16), "dp", scatter_dimension=0, tiled=True
        ).astype(jnp.float32),
    )
    gathered = (
        lax.all_gather(reduced[0].astype(jnp.bfloat16), "dp", axis=0, tiled=True).astype(
            jnp.float32
        ),
        lax.all_gather(reduced[1].astype(jnp.bfloat16), "dp", axis=0, tiled=True).astype(
            jnp.float32
        ),
        lax.all_gather(reduced[2].astype(jnp.bfloat16), "dp", axis=0, tiled=True).astype(
            jnp.float32
        ),
        lax.all_gather(reduced[3].astype(jnp.bfloat16), "dp", axis=1, tiled=True).astype(
            jnp.float32
        ),
        lax.all_gather(reduced[4].astype(jnp.bfloat16), "dp", axis=0, tiled=True).astype(
            jnp.float32
        ),
        lax.all_gather(reduced[5].astype(jnp.bfloat16), "dp", axis=0, tiled=True).astype(
            jnp.float32
        ),
        lax.all_gather(reduced[6].astype(jnp.bfloat16), "dp", axis=1, tiled=True).astype(
            jnp.float32
        ),
        lax.all_gather(reduced[7].astype(jnp.bfloat16), "dp", axis=0, tiled=True).astype(
            jnp.float32
        ),
    )
    return (
        output,
        input_grad,
        gathered[0],
        gathered[1],
        gathered[2],
        gathered[3],
        gathered[4],
        gathered[5],
        gathered[6],
        gain_attn_grad,
        gain_ffn_grad,
        gathered[7],
    )


def solution(mesh):
    return jax.shard_map(
        shards,
        mesh=mesh,
        in_specs=(
            P("dp", None, None),
            P("dp", None),
            P("dp", None, None),
            P(None, "tensor"),
            P(None, "tensor"),
            P(None, "tensor"),
            P("tensor", None),
            P(None, "tensor"),
            P(None, "tensor"),
            P("tensor", None),
            P(),
            P(),
            P(None, "tensor"),
        ),
        out_specs=(
            P("dp", "tensor", None),
            P("dp", "tensor", None),
            P(None, "tensor"),
            P(None, "tensor"),
            P(None, "tensor"),
            P("tensor", None),
            P(None, "tensor"),
            P(None, "tensor"),
            P("tensor", None),
            P(),
            P(),
            P(None, "tensor"),
        ),
        check_vma=False,
    )
```

profile of v0, /device:TPU:0, one launch (start us, length us, event | category | flops | bytes accessed | tf_op | source)
XLA Modules:
  0.0 1494.6 jit_solution(11549578221789818774)
XLA Ops:
  24.2 23.3 %fusion.1 = f32[524288,8]{0,1:T(8,128)} fusion(f32[32,8]{0,1:T(8,128)S(1)} %copy-done.45, s32[524288]{0:T(1024)S(1)} %fusion.51), kind=kOutput, calls=%fused_computation.2 | convolution fusion | flops 1627389952 | bytes 18875392 | tf_op jit(solution)/shard_map/dot_general | solution.py:105
  49.1 23.8 %fusion.3 = f32[524288,8]{0,1:T(8,128)} fusion(f32[32,8]{0,1:T(8,128)S(1)} %copy-done.45, s32[524288]{0:T(1024)S(1)} %fusion.50), kind=kOutput, calls=%fused_computation.5 | convolution fusion | flops 1627389952 | bytes 18875392 | tf_op jit(solution)/shard_map/dot_general | solution.py:105
  73.6 21.5 %fusion.84 = (f32[8,512]{1,0:T(8,128)S(1)}, f32[8,512,1024]{2,1,0:T(8,128)}) fusion(f32[1,8,512,1024]{3,1,2,0:T(8,128)} %bitcast.182, bf16[1024,8,64]{0,2,1:T(8,128)(2,1)S(1)} %bitcast.183, bf16[1,1024,8,64]{1,3,2,0:T(8,128)(2,1)S(1)} %bitcast.193, pred[512,1024]{1,0:T(8,128)(4,1)S(1)} %get-tuple-element.52), kind=kOutput, calls=%fused_computation.152 | convolution fusion | flops 549449728 | bytes 35667968 | tf_op jit(solution)/shard_map/qhd,khd->hqk/dot_general | solution.py:59
  109.6 21.5 %fusion.85 = (f32[8,512]{1,0:T(8,128)S(1)}, f32[8,512,1024]{2,1,0:T(8,128)}) fusion(f32[1,8,512,1024]{3,1,2,0:T(8,128)} %bitcast.181, bf16[1024,8,64]{0,2,1:T(8,128)(2,1)S(1)} %bitcast.184, bf16[1,1024,8,64]{1,3,2,0:T(8,128)(2,1)S(1)} %bitcast.194, pred[512,1024]{1,0:T(8,128)(4,1)S(1)} %get-tuple-element.51), kind=kOutput, calls=%fused_computation.153 | convolution fusion | flops 549449728 | bytes 35667968 | tf_op jit(solution)/shard_map/qhd,khd->hqk/dot_general | solution.py:59
  151.5 157.4 %all-reduce.7.cloned.1.call-done = bf16[1024,2048]{1,0:T(8,128)(2,1)} async-done(((bf16[1024,2048]{1,0:T(8,128)(2,1)}), bf16[1024,2048]{1,0:T(8,128)(2,1)}) %all-reduce.7.cloned.1.call-update) | async-done | bytes 4194320 | tf_op jit(solution)/shard_map/psum | solution.py:130
  324.9 11.4 multiply_convert_fusion.2
  336.4 13.3 fusion.32
  357.5 11.2 add_convert_fusion.1
  368.8 154.1 %all-reduce.9.cloned.1.call-done = bf16[1024,2048]{1,0:T(8,128)(2,1)} async-done(((bf16[1024,2048]{1,0:T(8,128)(2,1)}), bf16[1024,2048]{1,0:T(8,128)(2,1)}) %all-reduce.9.cloned.1.call-update) | async-done | bytes 4194320 | tf_op jit(solution)/shard_map/psum | solution.py:152
  531.1 10.1 multiply_add_fusion
  548.1 13.4 multiply_reduce_fusion.1
  580.0 18.7 %fusion.42 = (f32[1,8,512,1024]{3,2,1,0:T(8,128)}, bf16[8,512,1024]{2,1,0:T(8,128)(2,1)S(1)}) fusion(f32[8,512,1024]{2,1,0:T(8,128)} %get-tuple-element.68, f32[8,512]{1,0:T(8,128)S(1)} %get-tuple-element.67, f32[8,512,1024]{2,1,0:T(8,128)} %get-tuple-element.62, f32[8,512]{1,0:T(8,128)S(1)} %log_add_fusion.1), kind=kLoop, calls=%fused_computation.75 | loop fusion | flops 16777216 | bytes 58753024
  609.1 11.9 multiply_reduce_fusion
  621.0 19.4 %fusion.44 = (f32[1,8,512,1024]{3,2,1,0:T(8,128)}, bf16[8,512,1024]{2,1,0:T(8,128)(2,1)S(1)}) fusion(f32[8,512,1024]{2,1,0:T(8,128)} %get-tuple-element.66, f32[8,512]{1,0:T(8,128)S(1)} %get-tuple-element.65, f32[8,512,1024]{2,1,0:T(8,128)} %get-tuple-element.60, f32[8,512]{1,0:T(8,128)S(1)} %log_add_fusion), kind=kLoop, calls=%fused_computation.77 | loop fusion | flops 16777216 | bytes 58753024
  663.5 10.0 convolution_convert_fusion.2
  673.5 9.9 convolution_convert_fusion.1
  692.6 9.1 fusion.41
  712.7 42.1 %reduce-scatter.8.cloned.1.call-done = bf16[256,512]{1,0:T(8,128)(2,1)} async-done(((bf16[2048,512]{1,0:T(8,128)(2,1)}), bf16[256,512]{1,0:T(8,128)(2,1)}) %reduce-scatter.8.cloned.1.call-update) | async-done | bytes 262160 | tf_op jit(solution)/shard_map/reduce_scatter | solution.py:236
  754.9 10.4 convolution_convert_fusion.3
  776.5 38.9 %reduce-scatter.16.cloned.1.call-done = bf16[256,1280]{1,0:T(8,128)(2,1)} async-done(((bf16[2048,1280]{1,0:T(8,128)(2,1)}), bf16[256,1280]{1,0:T(8,128)(2,1)}) %reduce-scatter.16.cloned.1.call-update) | async-done | bytes 655376 | tf_op jit(solution)/shard_map/reduce_scatter | solution.py:248
  815.4 60.3 %reduce-scatter.18.cloned.1.call-done = bf16[256,1280]{1,0:T(8,128)(2,1)} async-done(((bf16[2048,1280]{1,0:T(8,128)(2,1)}), bf16[256,1280]{1,0:T(8,128)(2,1)}) %reduce-scatter.18.cloned.1.call-update) | async-done | bytes 655376 | tf_op jit(solution)/shard_map/reduce_scatter | solution.py:251
  875.8 59.9 %reduce-scatter.20.cloned.1.call-done = bf16[1280,256]{1,0:T(8,128)(2,1)} async-done(((bf16[1280,2048]{1,0:T(8,128)(2,1)}), bf16[1280,256]{1,0:T(8,128)(2,1)}) %reduce-scatter.20.cloned.1.call-update) | async-done | bytes 655376 | tf_op jit(solution)/shard_map/reduce_scatter | solution.py:254
  944.5 18.4 %copy.33 = f32[1,8,512,1024]{3,1,2,0:T(8,128)} copy(f32[1,8,512,1024]{3,2,1,0:T(8,128)} %get-tuple-element.40) | data formatting | bytes 33554432
  962.9 18.1 %copy.34 = f32[1,8,512,1024]{3,1,2,0:T(8,128)} copy(f32[1,8,512,1024]{3,2,1,0:T(8,128)} %get-tuple-element.42) | data formatting | bytes 33554432
  981.0 34.5 %fusion = f32[32,8]{1,0:T(8,128)S(1)} fusion(f32[8,524288]{1,0:T(8,128)} %bitcast.188, s32[524288]{0:T(1024)S(1)} %copy-done.21), kind=kOutput, calls=%fused_computation.1 | convolution fusion | flops 1627389952 | bytes 18875392 | tf_op jit(solution)/shard_map/dot_general | solution.py:212
  1015.5 34.6 %fusion.74 = bf16[32,8]{1,0:T(8,128)(2,1)S(1)} fusion(f32[32,8]{1,0:T(8,128)S(1)} %fusion, f32[8,524288]{1,0:T(8,128)} %bitcast.187, s32[524288]{0:T(1024)S(1)} %copy-done.23), kind=kOutput, calls=%fused_computation.129 | convolution fusion | flops 1627390464 | bytes 18875904 | tf_op jit(solution)/shard_map/dot_general | solution.py:212
  1050.2 12.6 all-reduce
  1062.9 9.7 all-gather
  1096.6 253.2 %all-reduce.11.cloned.1.call-done = (bf16[1024,2048]{1,0:T(8,128)(2,1)}, bf16[1024,2048]{1,0:T(8,128)(2,1)}) async-done(((bf16[1024,2048]{1,0:T(8,128)(2,1)}, bf16[1024,2048]{1,0:T(8,128)(2,1)}), (bf16[1024,2048]{1,0:T(8,128)(2,1)}, bf16[1024,2048]{1,0:T(8,128)(2,1)})) %all-reduce.11.cloned.1.call-update) | async-done | bytes 8388624 | tf_op jit(solution)/shard_map/psum | solution.py:138
  1368.6 39.7 %all-reduce.1 = (f32[2048]{0:T(1024)}, f32[2048]{0:T(1024)}) all-reduce(f32[2048]{0:T(1024)S(1)} %get-tuple-element.57, f32[2048]{0:T(1024)S(1)} %get-tuple-element.70), channel_id=1, replica_groups=mesh['dp'=8,'tensor'=4] {'dp','tensor'}, use_global_device_ids=true, to_apply=%region_22.23 | all-reduce | flops 4096 | bytes 32768 | tf_op jit(solution)/shard_map/psum | solution.py:234
  1415.6 20.0 %all-gather.19.cloned.1.call-done = bf16[2048,1280]{1,0:T(8,128)(2,1)} async-done(((bf16[256,1280]{1,0:T(8,128)(2,1)}), bf16[2048,1280]{1,0:T(8,128)(2,1)}) %all-gather.19.cloned.1.call-update) | async-done | bytes 5242896 | tf_op jit(solution)/shard_map/all_gather | solution.py:277
  1443.2 36.4 %all-gather.21.cloned.1.call-done = bf16[1280,2048]{1,0:T(8,128)(2,1)} async-done(((bf16[1280,256]{1,0:T(8,128)(2,1)}), bf16[1280,2048]{1,0:T(8,128)(2,1)}) %all-gather.21.cloned.1.call-update) | async-done | bytes 5242896 | tf_op jit(solution)/shard_map/all_gather | solution.py:280
  (236 shorter events, 250.0 us)
Async XLA Ops:
  7.2 139.4 %copy-start = (bf16[512,2048]{1,0:T(8,128)(2,1)S(1)}, bf16[512,2048]{1,0:T(8,128)(2,1)}, u32[]{:S(2)}) copy-start(bf16[512,2048]{1,0:T(8,128)(2,1)} %param.19) | copy-start | bytes 6291460
  7.2 301.7 %all-reduce.7.cloned.1.call-start = ((), (), s32[]{:S(2)}) async-start(), calls=%async_computation.7 | async-start | bytes 8388608 | tf_op jit(solution)/shard_map/psum | solution.py:130
  13.1 96.5 %copy-start.24 = (bf16[1024,512]{0,1:T(8,128)(2,1)}, bf16[1024,512]{0,1:T(8,128)(2,1)S(1)}, u32[]{:S(2)}) copy-start(bf16[1024,512]{0,1:T(8,128)(2,1)S(1)} %convolution_convert_fusion.10) | copy-start | bytes 3145732
  15.7 93.9 %copy-start.17 = (bf16[1024,512]{0,1:T(8,128)(2,1)}, bf16[1024,512]{0,1:T(8,128)(2,1)S(1)}, u32[]{:S(2)}) copy-start(bf16[1024,512]{0,1:T(8,128)(2,1)S(1)} %convolution_convert_fusion.9) | copy-start | bytes 3145732
  24.2 23.3 %copy-start.20 = (s32[524288]{0:T(1024)}, s32[524288]{0:T(1024)S(1)}, u32[]{:S(2)}) copy-start(s32[524288]{0:T(1024)S(1)} %fusion.51) | copy-start | bytes 6291460
  49.1 23.8 %copy-start.22 = (s32[524288]{0:T(1024)}, s32[524288]{0:T(1024)S(1)}, u32[]{:S(2)}) copy-start(s32[524288]{0:T(1024)S(1)} %fusion.50) | copy-start | bytes 6291460
  73.6 29.4 %copy-start.30 = (bf16[1024,512]{0,1:T(8,128)(2,1)S(1)}, bf16[1024,512]{0,1:T(8,128)(2,1)}, u32[]{:S(2)}) copy-start(bf16[1024,512]{0,1:T(8,128)(2,1)} %convolution_convert_fusion.11) | copy-start | bytes 3145732
  151.0 162.9 %copy-start.40 = (f32[2048]{0:T(1024)S(1)}, f32[2048]{0:T(1024)}, u32[]{:S(2)}) copy-start(f32[2048]{0:T(1024)} %param.24) | copy-start | bytes 24580
  151.1 371.8 %all-reduce.9.cloned.1.call-start = ((), (), s32[]{:S(2)}) async-start(), calls=%async_computation.8 | async-start | bytes 8388608 | tf_op jit(solution)/shard_map/psum | solution.py:152
  314.8 214.8 %copy-start.41 = (f32[1024]{0:T(1024)}, f32[1024]{0:T(1024)S(1)}, u32[]{:S(2)}) copy-start(f32[1024]{0:T(1024)S(1)} %add_rsqrt_fusion) | copy-start | bytes 12292
  317.6 18.7 %copy-start.26 = (bf16[1024,2048]{1,0:T(8,128)(2,1)}, bf16[1024,2048]{1,0:T(8,128)(2,1)S(1)}, u32[]{:S(2)}) copy-start(bf16[1024,2048]{1,0:T(8,128)(2,1)S(1)} %multiply_convert_fusion) | copy-start | bytes 12582916
  336.4 21.1 %copy-start.54 = (bf16[1024,1280]{1,0:T(8,128)(2,1)}, bf16[1024,1280]{1,0:T(8,128)(2,1)S(1)}, u32[]{:S(2)}) copy-start(bf16[1024,1280]{1,0:T(8,128)(2,1)S(1)} %get-tuple-element.63) | copy-start | bytes 7864324
  368.7 342.1 %reduce-scatter.12.cloned.1.call-start = ((), (), s32[]{:S(2)}) async-start(), calls=%async_computation.13 | async-start | bytes 2359296 | tf_op jit(solution)/shard_map/reduce_scatter | solution.py:242
  541.2 20.2 %slice-start = ((s8[16777216]{0:T(1024)(128)(4,1)}), s8[4194304]{0:T(1024)(128)(4,1)S(1)}, s32[]{:S(2)}) async-start(s8[16777216]{0:T(1024)(128)(4,1)} %bitcast.179), calls=%async_computation.24 | async-start | bytes 8388608
  541.2 20.2 %slice-start.1 = ((s8[16777216]{0:T(1024)(128)(4,1)}), s8[4194304]{0:T(1024)(128)(4,1)S(1)}, s32[]{:S(2)}) async-start(s8[16777216]{0:T(1024)(128)(4,1)} %bitcast.179), calls=%async_computation.25 | async-start | bytes 8388608
  579.9 131.4 %reduce-scatter.14.cloned.1.call-start = ((), (), s32[]{:S(2)}) async-start(), calls=%async_computation.15 | async-start | bytes 2359296 | tf_op jit(solution)/shard_map/reduce_scatter | solution.py:245
  580.0 18.7 %copy-start.25 = (bf16[1024,512]{0,1:T(8,128)(2,1)S(1)}, bf16[1024,512]{0,1:T(8,128)(2,1)}, u32[]{:S(2)}) copy-start(bf16[1024,512]{0,1:T(8,128)(2,1)} %copy-done.24) | copy-start | bytes 3145732
  621.0 91.1 %reduce-scatter.10.cloned.1.call-start = ((), (), s32[]{:S(2)}) async-start(), calls=%async_computation.11 | async-start | bytes 2359296 | tf_op jit(solution)/shard_map/reduce_scatter | solution.py:239
  650.0 104.8 %reduce-scatter.8.cloned.1.call-start = ((), (), s32[]{:S(2)}) async-start(), calls=%async_computation.9 | async-start | bytes 2359296 | tf_op jit(solution)/shard_map/reduce_scatter | solution.py:236
  663.4 151.9 %reduce-scatter.16.cloned.1.call-start = ((), (), s32[]{:S(2)}) async-start(), calls=%async_computation.17 | async-start | bytes 5898240 | tf_op jit(solution)/shard_map/reduce_scatter | solution.py:248
  673.5 202.2 %reduce-scatter.18.cloned.1.call-start = ((), (), s32[]{:S(2)}) async-start(), calls=%async_computation.19 | async-start | bytes 5898240 | tf_op jit(solution)/shard_map/reduce_scatter | solution.py:251
  683.5 252.3 %reduce-scatter.20.cloned.1.call-start = ((), (), s32[]{:S(2)}) async-start(), calls=%async_computation.21 | async-start | bytes 5898240 | tf_op jit(solution)/shard_map/reduce_scatter | solution.py:254
  710.7 369.1 %all-gather.13.cloned.1.call-start = ((), (), s32[]{:S(2)}) async-start(), calls=%async_computation.14 | async-start | bytes 2359296 | tf_op jit(solution)/shard_map/all_gather | solution.py:268
  711.3 372.7 %all-gather.15.cloned.1.call-start = ((), (), s32[]{:S(2)}) async-start(), calls=%async_computation.16 | async-start | bytes 2359296 | tf_op jit(solution)/shard_map/all_gather | solution.py:271
  712.0 376.1 %all-gather.11.cloned.1.call-start = ((), (), s32[]{:S(2)}) async-start(), calls=%async_computation.12 | async-start | bytes 2359296 | tf_op jit(solution)/shard_map/all_gather | solution.py:265
  712.6 379.7 %all-gather.9.cloned.1.call-start = ((), (), s32[]{:S(2)}) async-start(), calls=%async_computation.10 | async-start | bytes 2359296 | tf_op jit(solution)/shard_map/all_gather | solution.py:262
  754.8 595.0 %all-reduce.11.cloned.1.call-start = ((), (), s32[]{:S(2)}) async-start(), calls=%async_computation.23 | async-start | bytes 16777216 | tf_op jit(solution)/shard_map/psum | solution.py:138
  776.4 631.8 %all-gather.17.cloned.1.call-start = ((), (), s32[]{:S(2)}) async-start(), calls=%async_computation.18 | async-start | bytes 5898240 | tf_op jit(solution)/shard_map/all_gather | solution.py:274
  815.4 620.2 %all-gather.19.cloned.1.call-start = ((), (), s32[]{:S(2)}) async-start(), calls=%async_computation.20 | async-start | bytes 5898240 | tf_op jit(solution)/shard_map/all_gather | solution.py:277
  875.7 603.9 %all-gather.21.cloned.1.call-start = ((), (), s32[]{:S(2)}) async-start(), calls=%async_computation.22 | async-start | bytes 5898240 | tf_op jit(solution)/shard_map/all_gather | solution.py:280
  981.0 34.5 %copy-start.23 = (s32[524288]{0:T(1024)S(1)}, s32[524288]{0:T(1024)}, u32[]{:S(2)}) copy-start(s32[524288]{0:T(1024)} %copy-done.22) | copy-start | bytes 6291460
  1435.6 52.0 %copy-start.1 = (bf16[512,2048]{1,0:T(8,128)(2,1)S(1)}, bf16[512,2048]{1,0:T(8,128)(2,1)}, u32[]{:S(2)}) copy-start(bf16[512,2048]{1,0:T(8,128)(2,1)} %param.19) | copy-start | bytes 6291460
  (47 other events, 279.6 us)
Sparse Core Ops, SparseCore 0:
  151.2 157.6 all-reduce.6
  368.8 153.9 all-reduce.8
  580.1 40.2 reduce-scatter.11
  623.8 41.2 reduce-scatter.13
  668.2 41.2 reduce-scatter.9
  713.5 41.2 reduce-scatter.7
  758.7 56.5 reduce-scatter.15
  819.1 56.5 reduce-scatter.17
  879.1 56.5 reduce-scatter.19
  937.6 27.8 all-gather.12
  967.6 28.1 all-gather.14
  997.7 27.8 all-gather.10
  1027.7 27.9 all-gather.8
  1058.3 291.5 all-reduce.10
  1351.7 40.4 all-gather.16
  1394.1 41.4 all-gather.18
  1437.5 42.0 all-gather.20
where the time goes:
time: 1500 us; the launch traced here: 1490 us
  waiting for transfers between devices  824 us (55%)
  matrix products  375 us (25%)
  other arithmetic  155 us (10%)
  blocking collectives  62 us (4%)
  local copies, waits for them, and re-layouts  61.4 us (4%)
  between operations  15.9 us (1%)
    psum x1, waiting for transfers between devices, shards(): lax.psum(ffn_part.astype(jnp.bfloat16), 'tensor').astype(jnp.float32)  253 us
    psum x1, waiting for transfers between devices, shards(): lax.psum(attn_part.astype(jnp.bfloat16), 'tensor').astype(jnp.float32)  157 us
    psum x1, waiting for transfers between devices, shards(): lax.psum(norm_ffn_part.astype(jnp.bfloat16), 'tensor').astype(jnp.float32)  154 us
    dot_general x2, matrix products, shards(): lax.dot_general(onehot, score_sums[block_index].reshape(head_count, block...  69.2 us
    dot_general x9, matrix products, project(): return jnp.dot(left_side, right_side, preferred_element_type=jnp.float32)  62.2 us
    unnamed x133, local copies, waits for them, and re-layouts  60.4 us
    reduce_scatter x1, waiting for transfers between devices, shards(): lax.psum_scatter(up_grad.astype(jnp.bfloat16), 'dp', scatter_dimension=0,...  60.3 us
    reduce_scatter x1, waiting for transfers between devices, shards(): lax.psum_scatter(down_grad.astype(jnp.bfloat16), 'dp', scatter_dimension=...  59.9 us
  transfers between devices with their start and end apart: 17, of which 9 were waited for; matrix products, arithmetic and copies ran while one was open for 21% of the time, Pallas kernels for 0%

commit v1 on v0

--- a/solution.py
+++ b/solution.py
@@ -5,6 +5,18 @@
 
 thresholds = (12, 16, 23, 32, 46, 64, 91)
 highest = lax.Precision.HIGHEST
+
+
+def collect(array, axis, dim):
+    ways, here = (lax.axis_size(axis), lax.axis_index(axis))
+    grown, reach = (array, 1)
+    while reach < ways:
+        theirs = lax.ppermute(grown, axis, [(d, d ^ reach) for d in range(ways)])
+        mine_first = jnp.concatenate([grown, theirs], axis=dim)
+        theirs_first = jnp.concatenate([theirs, grown], axis=dim)
+        grown = jnp.where(here & reach == 0, mine_first, theirs_first)
+        reach = 2 * reach
+    return grown
 
 
 def buckets_of(start_row, query_count, length):
@@ -277,9 +289,7 @@
         lax.all_gather(reduced[5].astype(jnp.bfloat16), "dp", axis=0, tiled=True).astype(
             jnp.float32
         ),
-        lax.all_gather(reduced[6].astype(jnp.bfloat16), "dp", axis=1, tiled=True).astype(
-            jnp.float32
-        ),
+        collect(reduced[6].astype(jnp.bfloat16), "dp", 1).astype(jnp.float32),
         lax.all_gather(reduced[7].astype(jnp.bfloat16), "dp", axis=0, tiled=True).astype(
             jnp.float32
         ),

time: 1500 us -> 1480 us (0.987)
  waiting for transfers between devices: 824 us -> 796 us
    all_gather x1 -> x0, waiting for transfers between devices: 36.4 us -> none  [shards(): lax.all_gather(reduced[6].astype(jnp.bfloat16), 'dp', axis=1, tiled=True)]
  transfers between devices with their start and end apart: 17 -> 19, of which waited for: 9 -> 9; matrix products, arithmetic and copies ran while one was open for 21% -> 22% of each run, Pallas kernels for 0% -> 0%
where the time goes in v1:
time: 1480 us; the launch traced here: 1470 us
  waiting for transfers between devices  796 us (54%)
  matrix products  375 us (25%)
  other arithmetic  163 us (11%)
  blocking collectives  61.4 us (4%)
  local copies, waits for them, and re-layouts  60.9 us (4%)
  between operations  15.9 us (1%)
    psum x1, waiting for transfers between devices, shards(): lax.psum(ffn_part.astype(jnp.bfloat16), 'tensor').astype(jnp.float32)  258 us
    psum x1, waiting for transfers between devices, shards(): lax.psum(attn_part.astype(jnp.bfloat16), 'tensor').astype(jnp.float32)  157 us
    psum x1, waiting for transfers between devices, shards(): lax.psum(norm_ffn_part.astype(jnp.bfloat16), 'tensor').astype(jnp.float32)  154 us
    dot_general x2, matrix products, shards(): lax.dot_general(onehot, score_sums[block_index].reshape(head_count, block...  69 us
    dot_general x9, matrix products, project(): return jnp.dot(left_side, right_side, preferred_element_type=jnp.float32)  62.2 us
    reduce_scatter x1, waiting for transfers between devices, shards(): lax.psum_scatter(up_grad.astype(jnp.bfloat16), 'dp', scatter_dimension=0,...  60.9 us
    reduce_scatter x1, waiting for transfers between devices, shards(): lax.psum_scatter(down_grad.astype(jnp.bfloat16), 'dp', scatter_dimension=...  60 us
    unnamed x133, local copies, waits for them, and re-layouts  59.9 us
  transfers between devices with their start and end apart: 19, of which 9 were waited for; matrix products, arithmetic and copies ran while one was open for 22% of the time, Pallas kernels for 0%

profile of v1, /device:TPU:0, one launch (start us, length us, event | category | flops | bytes accessed | tf_op | source)
XLA Modules:
  0.0 1474.8 jit_solution(17218551931943799460)
XLA Ops:
  24.2 23.2 %fusion.1 = f32[524288,8]{0,1:T(8,128)} fusion(f32[32,8]{0,1:T(8,128)S(1)} %copy-done.45, s32[524288]{0:T(1024)S(1)} %fusion.52), kind=kOutput, calls=%fused_computation.2 | convolution fusion | flops 1627389952 | bytes 18875392 | tf_op jit(solution)/shard_map/dot_general | solution.py:117
  49.1 23.6 %fusion.3 = f32[524288,8]{0,1:T(8,128)} fusion(f32[32,8]{0,1:T(8,128)S(1)} %copy-done.45, s32[524288]{0:T(1024)S(1)} %fusion.51), kind=kOutput, calls=%fused_computation.5 | convolution fusion | flops 1627389952 | bytes 18875392 | tf_op jit(solution)/shard_map/dot_general | solution.py:117
  73.4 21.6 %fusion.85 = (f32[8,512]{1,0:T(8,128)S(1)}, f32[8,512,1024]{2,1,0:T(8,128)}) fusion(f32[1,8,512,1024]{3,1,2,0:T(8,128)} %bitcast.182, bf16[1024,8,64]{0,2,1:T(8,128)(2,1)S(1)} %bitcast.183, bf16[1,1024,8,64]{1,3,2,0:T(8,128)(2,1)S(1)} %bitcast.193, pred[512,1024]{1,0:T(8,128)(4,1)S(1)} %get-tuple-element.52), kind=kOutput, calls=%fused_computation.156 | convolution fusion | flops 549449728 | bytes 35667968 | tf_op jit(solution)/shard_map/qhd,khd->hqk/dot_general | solution.py:71
  109.4 21.5 %fusion.86 = (f32[8,512]{1,0:T(8,128)S(1)}, f32[8,512,1024]{2,1,0:T(8,128)}) fusion(f32[1,8,512,1024]{3,1,2,0:T(8,128)} %bitcast.181, bf16[1024,8,64]{0,2,1:T(8,128)(2,1)S(1)} %bitcast.184, bf16[1,1024,8,64]{1,3,2,0:T(8,128)(2,1)S(1)} %bitcast.194, pred[512,1024]{1,0:T(8,128)(4,1)S(1)} %get-tuple-element.51), kind=kOutput, calls=%fused_computation.157 | convolution fusion | flops 549449728 | bytes 35667968 | tf_op jit(solution)/shard_map/qhd,khd->hqk/dot_general | solution.py:71
  151.4 157.4 %all-reduce.7.cloned.1.call-done = bf16[1024,2048]{1,0:T(8,128)(2,1)} async-done(((bf16[1024,2048]{1,0:T(8,128)(2,1)}), bf16[1024,2048]{1,0:T(8,128)(2,1)}) %all-reduce.7.cloned.1.call-update) | async-done | bytes 4194320 | tf_op jit(solution)/shard_map/psum | solution.py:142
  324.9 11.4 multiply_convert_fusion.2
  336.3 13.3 fusion.32
  357.4 11.2 add_convert_fusion.1
  368.7 154.1 %all-reduce.9.cloned.1.call-done = bf16[1024,2048]{1,0:T(8,128)(2,1)} async-done(((bf16[1024,2048]{1,0:T(8,128)(2,1)}), bf16[1024,2048]{1,0:T(8,128)(2,1)}) %all-reduce.9.cloned.1.call-update) | async-done | bytes 4194320 | tf_op jit(solution)/shard_map/psum | solution.py:164
  531.1 10.1 multiply_add_fusion
  548.0 13.4 multiply_reduce_fusion.1
  579.9 18.7 %fusion.43 = (f32[1,8,512,1024]{3,2,1,0:T(8,128)}, bf16[8,512,1024]{2,1,0:T(8,128)(2,1)S(1)}) fusion(f32[8,512,1024]{2,1,0:T(8,128)} %get-tuple-element.68, f32[8,512]{1,0:T(8,128)S(1)} %get-tuple-element.67, f32[8,512,1024]{2,1,0:T(8,128)} %get-tuple-element.62, f32[8,512]{1,0:T(8,128)S(1)} %log_add_fusion.1), kind=kLoop, calls=%fused_computation.77 | loop fusion | flops 16777216 | bytes 58753024
  609.0 11.8 multiply_reduce_fusion
  620.9 19.4 %fusion.45 = (f32[1,8,512,1024]{3,2,1,0:T(8,128)}, bf16[8,512,1024]{2,1,0:T(8,128)(2,1)S(1)}) fusion(f32[8,512,1024]{2,1,0:T(8,128)} %get-tuple-element.66, f32[8,512]{1,0:T(8,128)S(1)} %get-tuple-element.65, f32[8,512,1024]{2,1,0:T(8,128)} %get-tuple-element.60, f32[8,512]{1,0:T(8,128)S(1)} %log_add_fusion), kind=kLoop, calls=%fused_computation.79 | loop fusion | flops 16777216 | bytes 58753024
  663.3 10.0 convolution_convert_fusion.2
  673.4 9.9 convolution_convert_fusion.1
  692.5 9.1 fusion.41
  712.5 42.2 %reduce-scatter.8.cloned.1.call-done = bf16[256,512]{1,0:T(8,128)(2,1)} async-done(((bf16[2048,512]{1,0:T(8,128)(2,1)}), bf16[256,512]{1,0:T(8,128)(2,1)}) %reduce-scatter.8.cloned.1.call-update) | async-done | bytes 262160 | tf_op jit(solution)/shard_map/reduce_scatter | solution.py:248
  754.8 10.4 convolution_convert_fusion.3
  776.5 38.7 %reduce-scatter.16.cloned.1.call-done = bf16[256,1280]{1,0:T(8,128)(2,1)} async-done(((bf16[2048,1280]{1,0:T(8,128)(2,1)}), bf16[256,1280]{1,0:T(8,128)(2,1)}) %reduce-scatter.16.cloned.1.call-update) | async-done | bytes 655376 | tf_op jit(solution)/shard_map/reduce_scatter | solution.py:260
  815.3 60.9 %reduce-scatter.18.cloned.1.call-done = bf16[256,1280]{1,0:T(8,128)(2,1)} async-done(((bf16[2048,1280]{1,0:T(8,128)(2,1)}), bf16[256,1280]{1,0:T(8,128)(2,1)}) %reduce-scatter.18.cloned.1.call-update) | async-done | bytes 655376 | tf_op jit(solution)/shard_map/reduce_scatter | solution.py:263
  876.2 60.0 %reduce-scatter.20.cloned.1.call-done = bf16[1280,256]{1,0:T(8,128)(2,1)} async-done(((bf16[1280,2048]{1,0:T(8,128)(2,1)}), bf16[1280,256]{1,0:T(8,128)(2,1)}) %reduce-scatter.20.cloned.1.call-update) | async-done | bytes 655376 | tf_op jit(solution)/shard_map/reduce_scatter | solution.py:266
  950.3 18.2 %copy.33 = f32[1,8,512,1024]{3,1,2,0:T(8,128)} copy(f32[1,8,512,1024]{3,2,1,0:T(8,128)} %get-tuple-element.40) | data formatting | bytes 33554432
  968.5 17.7 %copy.34 = f32[1,8,512,1024]{3,1,2,0:T(8,128)} copy(f32[1,8,512,1024]{3,2,1,0:T(8,128)} %get-tuple-element.42) | data formatting | bytes 33554432
  990.5 34.5 %fusion = f32[32,8]{1,0:T(8,128)S(1)} fusion(f32[8,524288]{1,0:T(8,128)} %bitcast.188, s32[524288]{0:T(1024)S(1)} %copy-done.21), kind=kOutput, calls=%fused_computation.1 | convolution fusion | flops 1627389952 | bytes 18875392 | tf_op jit(solution)/shard_map/dot_general | solution.py:224
  1025.0 34.5 %fusion.75 = bf16[32,8]{1,0:T(8,128)(2,1)S(1)} fusion(f32[32,8]{1,0:T(8,128)S(1)} %fusion, f32[8,524288]{1,0:T(8,128)} %bitcast.187, s32[524288]{0:T(1024)S(1)} %copy-done.23), kind=kOutput, calls=%fused_computation.133 | convolution fusion | flops 1627390464 | bytes 18875904 | tf_op jit(solution)/shard_map/dot_general | solution.py:224
  1059.5 12.8 all-reduce
  1072.3 9.0 all-gather
  1105.6 10.8 fusion.42
  1116.4 258.3 %all-reduce.11.cloned.1.call-done = (bf16[1024,2048]{1,0:T(8,128)(2,1)}, bf16[1024,2048]{1,0:T(8,128)(2,1)}) async-done(((bf16[1024,2048]{1,0:T(8,128)(2,1)}, bf16[1024,2048]{1,0:T(8,128)(2,1)}), (bf16[1024,2048]{1,0:T(8,128)(2,1)}, bf16[1024,2048]{1,0:T(8,128)(2,1)})) %all-reduce.11.cloned.1.call-update) | async-done | bytes 8388624 | tf_op jit(solution)/shard_map/psum | solution.py:150
  1393.2 39.6 %all-reduce.1 = (f32[2048]{0:T(1024)}, f32[2048]{0:T(1024)}) all-reduce(f32[2048]{0:T(1024)S(1)} %get-tuple-element.57, f32[2048]{0:T(1024)S(1)} %get-tuple-element.70), channel_id=1, replica_groups=mesh['dp'=8,'tensor'=4] {'dp','tensor'}, use_global_device_ids=true, to_apply=%region_22.23 | all-reduce | flops 4096 | bytes 32768 | tf_op jit(solution)/shard_map/psum | solution.py:246
  1440.4 20.1 %all-gather.18.cloned.1.call-done = bf16[2048,1280]{1,0:T(8,128)(2,1)} async-done(((bf16[256,1280]{1,0:T(8,128)(2,1)}), bf16[2048,1280]{1,0:T(8,128)(2,1)}) %all-gather.18.cloned.1.call-update) | async-done | bytes 5242896 | tf_op jit(solution)/shard_map/all_gather | solution.py:289
  (241 shorter events, 251.6 us)
Async XLA Ops:
  7.2 139.4 %copy-start = (bf16[512,2048]{1,0:T(8,128)(2,1)S(1)}, bf16[512,2048]{1,0:T(8,128)(2,1)}, u32[]{:S(2)}) copy-start(bf16[512,2048]{1,0:T(8,128)(2,1)} %param.19) | copy-start | bytes 6291460
  7.2 301.6 %all-reduce.7.cloned.1.call-start = ((), (), s32[]{:S(2)}) async-start(), calls=%async_computation.7 | async-start | bytes 8388608 | tf_op jit(solution)/shard_map/psum | solution.py:142
  13.1 96.3 %copy-start.24 = (bf16[1024,512]{0,1:T(8,128)(2,1)}, bf16[1024,512]{0,1:T(8,128)(2,1)S(1)}, u32[]{:S(2)}) copy-start(bf16[1024,512]{0,1:T(8,128)(2,1)S(1)} %convolution_convert_fusion.10) | copy-start | bytes 3145732
  15.7 93.7 %copy-start.17 = (bf16[1024,512]{0,1:T(8,128)(2,1)}, bf16[1024,512]{0,1:T(8,128)(2,1)S(1)}, u32[]{:S(2)}) copy-start(bf16[1024,512]{0,1:T(8,128)(2,1)S(1)} %convolution_convert_fusion.9) | copy-start | bytes 3145732
  24.2 23.3 %copy-start.20 = (s32[524288]{0:T(1024)}, s32[524288]{0:T(1024)S(1)}, u32[]{:S(2)}) copy-start(s32[524288]{0:T(1024)S(1)} %fusion.52) | copy-start | bytes 6291460
  49.1 23.6 %copy-start.22 = (s32[524288]{0:T(1024)}, s32[524288]{0:T(1024)S(1)}, u32[]{:S(2)}) copy-start(s32[524288]{0:T(1024)S(1)} %fusion.51) | copy-start | bytes 6291460
  73.4 29.4 %copy-start.30 = (bf16[1024,512]{0,1:T(8,128)(2,1)S(1)}, bf16[1024,512]{0,1:T(8,128)(2,1)}, u32[]{:S(2)}) copy-start(bf16[1024,512]{0,1:T(8,128)(2,1)} %convolution_convert_fusion.11) | copy-start | bytes 3145732
  151.0 162.9 %copy-start.40 = (f32[2048]{0:T(1024)S(1)}, f32[2048]{0:T(1024)}, u32[]{:S(2)}) copy-start(f32[2048]{0:T(1024)} %param.24) | copy-start | bytes 24580
  151.0 371.8 %all-reduce.9.cloned.1.call-start = ((), (), s32[]{:S(2)}) async-start(), calls=%async_computation.8 | async-start | bytes 8388608 | tf_op jit(solution)/shard_map/psum | solution.py:164
  314.7 214.8 %copy-start.41 = (f32[1024]{0:T(1024)}, f32[1024]{0:T(1024)S(1)}, u32[]{:S(2)}) copy-start(f32[1024]{0:T(1024)S(1)} %add_rsqrt_fusion) | copy-start | bytes 12292
  336.3 21.1 %copy-start.54 = (bf16[1024,1280]{1,0:T(8,128)(2,1)}, bf16[1024,1280]{1,0:T(8,128)(2,1)S(1)}, u32[]{:S(2)}) copy-start(bf16[1024,1280]{1,0:T(8,128)(2,1)S(1)} %get-tuple-element.63) | copy-start | bytes 7864324
  368.6 342.0 %reduce-scatter.12.cloned.1.call-start = ((), (), s32[]{:S(2)}) async-start(), calls=%async_computation.13 | async-start | bytes 2359296 | tf_op jit(solution)/shard_map/reduce_scatter | solution.py:254
  541.2 20.2 %slice-start = ((s8[16777216]{0:T(1024)(128)(4,1)}), s8[4194304]{0:T(1024)(128)(4,1)S(1)}, s32[]{:S(2)}) async-start(s8[16777216]{0:T(1024)(128)(4,1)} %bitcast.179), calls=%async_computation.23 | async-start | bytes 8388608
  541.2 20.2 %slice-start.1 = ((s8[16777216]{0:T(1024)(128)(4,1)}), s8[4194304]{0:T(1024)(128)(4,1)S(1)}, s32[]{:S(2)}) async-start(s8[16777216]{0:T(1024)(128)(4,1)} %bitcast.179), calls=%async_computation.24 | async-start | bytes 8388608
  579.8 131.4 %reduce-scatter.14.cloned.1.call-start = ((), (), s32[]{:S(2)}) async-start(), calls=%async_computation.15 | async-start | bytes 2359296 | tf_op jit(solution)/shard_map/reduce_scatter | solution.py:257
  620.8 91.1 %reduce-scatter.10.cloned.1.call-start = ((), (), s32[]{:S(2)}) async-start(), calls=%async_computation.11 | async-start | bytes 2359296 | tf_op jit(solution)/shard_map/reduce_scatter | solution.py:251
  649.9 104.8 %reduce-scatter.8.cloned.1.call-start = ((), (), s32[]{:S(2)}) async-start(), calls=%async_computation.9 | async-start | bytes 2359296 | tf_op jit(solution)/shard_map/reduce_scatter | solution.py:248
  663.3 151.9 %reduce-scatter.16.cloned.1.call-start = ((), (), s32[]{:S(2)}) async-start(), calls=%async_computation.17 | async-start | bytes 5898240 | tf_op jit(solution)/shard_map/reduce_scatter | solution.py:260
  673.3 202.8 %reduce-scatter.18.cloned.1.call-start = ((), (), s32[]{:S(2)}) async-start(), calls=%async_computation.19 | async-start | bytes 5898240 | tf_op jit(solution)/shard_map/reduce_scatter | solution.py:263
  683.3 252.8 %reduce-scatter.20.cloned.1.call-start = ((), (), s32[]{:S(2)}) async-start(), calls=%async_computation.21 | async-start | bytes 5898240 | tf_op jit(solution)/shard_map/reduce_scatter | solution.py:266
  710.5 378.1 %all-gather.12.cloned.1.call-start = ((), (), s32[]{:S(2)}) async-start(), calls=%async_computation.14 | async-start | bytes 2359296 | tf_op jit(solution)/shard_map/all_gather | solution.py:280
  711.1 381.9 %all-gather.14.cloned.1.call-start = ((), (), s32[]{:S(2)}) async-start(), calls=%async_computation.16 | async-start | bytes 2359296 | tf_op jit(solution)/shard_map/all_gather | solution.py:283
  711.9 385.3 %all-gather.10.cloned.1.call-start = ((), (), s32[]{:S(2)}) async-start(), calls=%async_computation.12 | async-start | bytes 2359296 | tf_op jit(solution)/shard_map/all_gather | solution.py:277
  712.4 389.0 %all-gather.8.cloned.1.call-start = ((), (), s32[]{:S(2)}) async-start(), calls=%async_computation.10 | async-start | bytes 2359296 | tf_op jit(solution)/shard_map/all_gather | solution.py:274
  754.7 620.0 %all-reduce.11.cloned.1.call-start = ((), (), s32[]{:S(2)}) async-start(), calls=%async_computation.22 | async-start | bytes 16777216 | tf_op jit(solution)/shard_map/psum | solution.py:150
  776.5 656.4 %all-gather.16.cloned.1.call-start = ((), (), s32[]{:S(2)}) async-start(), calls=%async_computation.18 | async-start | bytes 5898240 | tf_op jit(solution)/shard_map/all_gather | solution.py:286
  815.2 645.2 %all-gather.18.cloned.1.call-start = ((), (), s32[]{:S(2)}) async-start(), calls=%async_computation.20 | async-start | bytes 5898240 | tf_op jit(solution)/shard_map/all_gather | solution.py:289
  936.2 2.3 collective-permute-start
  940.1 46.1 %collective-permute-start.1 = (bf16[1280,512]{1,0:T(8,128)(2,1)S(1)}, bf16[1280,512]{1,0:T(8,128)(2,1)}, u32[]{:S(2)}, u32[]{:S(2)}) collective-permute-start(bf16[1280,512]{1,0:T(8,128)(2,1)S(1)} %maximum_select_fusion.2), channel_id=1, source_target_pairs={{0,8},{4,12},{8,0},{12,4},{16,24},{20,28},{24,16},{28,20},{1,9},{5... | collective-permute-start | bytes 3932168 | tf_op jit(solution)/shard_map/ppermute | solution.py:14
  989.9 115.7 %collective-permute-start.2 = (bf16[1280,1024]{1,0:T(8,128)(2,1)}, bf16[1280,1024]{1,0:T(8,128)(2,1)}, u32[]{:S(2)}, u32[]{:S(2)}) collective-permute-start(bf16[1280,1024]{1,0:T(8,128)(2,1)} %maximum_select_fusion.1), channel_id=1, source_target_pairs={{0,16},{4,20},{8,24},{12,28},{16,0},{20,4},{24,8},{28,12},{1,17},{... | collective-permute-start | bytes 7864328 | tf_op jit(solution)/shard_map/ppermute | solution.py:14
  990.5 34.5 %copy-start.23 = (s32[524288]{0:T(1024)S(1)}, s32[524288]{0:T(1024)}, u32[]{:S(2)}) copy-start(s32[524288]{0:T(1024)} %copy-done.22) | copy-start | bytes 6291460
  1432.8 35.0 %copy-start.1 = (bf16[512,2048]{1,0:T(8,128)(2,1)S(1)}, bf16[512,2048]{1,0:T(8,128)(2,1)}, u32[]{:S(2)}) copy-start(bf16[512,2048]{1,0:T(8,128)(2,1)} %param.19) | copy-start | bytes 6291460
  (49 other events, 303.2 us)
Sparse Core Ops, SparseCore 0:
  151.1 157.6 all-reduce.6
  368.7 153.9 all-reduce.8
  579.9 40.2 reduce-scatter.11
  623.7 41.2 reduce-scatter.13
  668.1 41.1 reduce-scatter.9
  713.4 41.2 reduce-scatter.7
  758.6 56.5 reduce-scatter.15
  819.5 56.5 reduce-scatter.17
  879.6 56.5 reduce-scatter.19
  938.0 36.3 all-gather.11
  976.5 33.9 all-gather.13
  1012.4 36.6 all-gather.9
  1051.1 29.3 all-gather.7
  1083.1 291.5 all-reduce.10
  1376.6 40.4 all-gather.15
  1419.0 41.4 all-gather.17
